TPU v7x, 32 devices: a whole 2x2x4 slice. The times are simulated.
32 devices in a mesh: grp: 2 (over y), tm: 8 (over z, x), row: 2 (over core).
Axes of the slice: x: 2, y: 2, z: 4, core: 2. Of those that a mesh axis runs over, the one named last changes fastest.
Arguments:
- queries: bfloat16 [4096, 768], P(('grp', 'tm', 'row')), parts along dimension 0, may hold values from -5 to 5
- keys: bfloat16 [4096, 768], P(('grp', 'tm', 'row')), parts along dimension 0, may hold values from -5 to 5
- values: bfloat16 [4096, 768], P(('grp', 'tm', 'row')), parts along dimension 0, may hold values from -6 to 6
- d_out: bfloat16 [4096, 768], P(('grp', 'tm', 'row')), parts along dimension 0, may hold values from -6 to 6
- action_table: bfloat16 [8, 768], replicated, may hold values from -5 to 5
- actions: int32 [16], P(('grp', 'tm')), parts along dimension 0, may hold values from 0 to 7
- temporal_list: int32 [32, 2], P(('grp', 'tm', 'row')), parts along dimension 0, may hold values from 1 to 3, as said below
Outputs:
- attended: bfloat16 [4096, 768], P(('grp', 'tm', 'row')), parts along dimension 0
- grad_queries: bfloat16 [4096, 768], P(('grp', 'tm', 'row')), parts along dimension 0
- grad_keys: bfloat16 [4096, 768], P(('grp', 'tm', 'row')), parts along dimension 0
- grad_values: bfloat16 [4096, 768], P(('grp', 'tm', 'row')), parts along dimension 0
- grad_table: float32 [16, 768], P('grp'), parts along dimension 0
There are 2 independent parts, one for each index of `grp`. A program takes and returns all parts, laid end to end along the dimension named above; an argument that names none is the same for every part. Nothing has to cross between parts.
Inputs may be any that keep to these rules, and one draw needn't show every extreme that they name: `temporal_list`: row b lists, in rising order, 2 different frame distances of 1 to 3.
All inputs are finite; a program needn't handle non-finite values.
Results may differ from a plain program's by a relative error of at most 0.012.
Values may be sent and summed in bfloat16 or wider, within the bound.
No kernel may reach another device: no remote copies, remote signals or barrier semaphores. Data moves between devices by JAX's collectives and lax.ppermute only.
A program may use at most 64 MiB of HBM per device.

v0:
```python
import math
import jax
import jax.numpy as jnp
from jax import lax
from jax.sharding import PartitionSpec as P

HEADS = 8
HEAD_DIM = 96
DIST = 3
LIST = 2


def from_behind(block, axis, distance):
    devices = range(lax.axis_size(axis))
    route = [(i - distance, i) for i in devices if i - distance in devices]
    return lax.ppermute(block, axis, route)


def attention_pass(queries, key_set, value_set, allowed, d_out):
    query_rows = queries.shape[0]
    key_rows = key_set.shape[0]
    model_width = queries.shape[1]
    score_scale = 1.0 / math.sqrt(HEAD_DIM)
    query_heads = queries.reshape(query_rows, HEADS, HEAD_DIM)
    key_heads = key_set.reshape(key_rows, HEADS, HEAD_DIM)
    value_heads = value_set.reshape(key_rows, HEADS, HEAD_DIM)
    grad_heads = d_out.reshape(query_rows, HEADS, HEAD_DIM)
    scores = (
        jnp.einsum("qhd,khd->hqk", query_heads, key_heads, preferred_element_type=jnp.float32)
        * score_scale
    )
    scores = jnp.where(allowed[None, None, :], scores, -1e30)
    highest = jnp.max(scores, axis=2, keepdims=True)
    weights = jnp.where(allowed[None, None, :], jnp.exp(scores - highest), 0.0)
    totals = jnp.sum(weights, axis=2, keepdims=True)
    probabilities = weights / totals
    log_total = (highest + jnp.log(totals))[:, :, 0].T
    probs_low = probabilities.astype(jnp.bfloat16)
    out_full = jnp.einsum(
        "hqk,khd->qhd", probs_low, value_heads, preferred_element_type=jnp.float32
    )
    d_probs = jnp.einsum(
        "qhd,khd->hqk", grad_heads, value_heads, preferred_element_type=jnp.float32
    )
    centre = jnp.sum(grad_heads.astype(jnp.float32) * out_full, axis=2)
    d_scores = (probabilities * (d_probs - centre.T[:, :, None])).astype(jnp.bfloat16)
    grad_query = (
        jnp.einsum("hqk,khd->qhd", d_scores, key_heads, preferred_element_type=jnp.float32)
        * score_scale
    )
    grad_key = None
    grad_value = None
    grad_key = (
        jnp.einsum(
            "hqk,qhd->khd", d_scores, query_heads, preferred_element_type=jnp.float32
        ).reshape(key_rows, model_width)
        * score_scale
    )
    grad_value = jnp.einsum(
        "hqk,qhd->khd", probs_low, grad_heads, preferred_element_type=jnp.float32
    ).reshape(key_rows, model_width)
    return (
        out_full.reshape(query_rows, model_width),
        grad_query.reshape(query_rows, model_width),
        grad_key,
        grad_value,
        log_total,
        centre,
    )


def on_device(queries, keys, values, d_out, action_table, actions, temporal_list):
    block_rows = queries.shape[0]
    model_width = queries.shape[1]
    frame_index = lax.axis_index("tm")
    labels = lax.iota(jnp.int32, action_table.shape[0])
    matches = actions[0] == labels
    action_row = jnp.dot(
        matches.astype(jnp.bfloat16)[None, :], action_table, preferred_element_type=jnp.float32
    )
    cond_values = (values.astype(jnp.float32) + action_row).astype(jnp.bfloat16)
    own_pair = jnp.stack([keys, cond_values])
    frame_pair = lax.all_gather(own_pair, "row", axis=1, tiled=True)
    earlier = []
    moving = own_pair
    for distance in range(DIST):
        moving = from_behind(moving, "tm", 1)
        earlier.append(moving)
    stacked = jnp.stack(earlier)
    distances = temporal_list[0]
    chosen = jnp.take(stacked, distances - 1, axis=0)
    frame_tokens = frame_pair.shape[1]
    key_set = jnp.concatenate(
        [frame_pair[0], chosen[:, 0].reshape(LIST * block_rows, model_width)], axis=0
    )
    value_set = jnp.concatenate(
        [frame_pair[1], chosen[:, 1].reshape(LIST * block_rows, model_width)], axis=0
    )
    present = frame_index - distances >= 0
    allowed = jnp.concatenate(
        [jnp.ones((frame_tokens,), dtype=bool), jnp.repeat(present, block_rows)]
    )
    out_full, grad_query, grad_key, grad_value, log_total, centre = attention_pass(
        queries, key_set, value_set, allowed, d_out
    )
    frame_terms = jnp.stack([grad_key[:frame_tokens], grad_value[:frame_tokens]])
    frame_grads = lax.psum_scatter(frame_terms, "row", scatter_dimension=1, tiled=True)
    slot_grads = []
    for listed in range(LIST):
        first_row = frame_tokens + listed * block_rows
        slot_grads.append(
            jnp.stack(
                [
                    grad_key[first_row : first_row + block_rows],
                    grad_value[first_row : first_row + block_rows],
                ]
            )
        )
    partials = []
    for distance in range(DIST):
        summed = jnp.zeros((2, block_rows, model_width), jnp.float32)
        for listed in range(LIST):
            summed = summed + jnp.where(distances[listed] == distance + 1, slot_grads[listed], 0.0)
        partials.append(summed)
    carried = jnp.zeros_like(partials[0])
    for distance in reversed(range(DIST)):
        carried = from_behind(carried + partials[distance], "tm", -1)
    key_total = frame_grads[0] + carried[0]
    value_total = frame_grads[1] + carried[1]
    column_sums = jnp.sum(value_total, axis=0)
    local_table = jnp.where(matches[:, None], column_sums[None, :], 0.0)
    grad_table = lax.psum(local_table, ("tm", "row"))
    return (
        out_full.astype(jnp.bfloat16),
        grad_query.astype(jnp.bfloat16),
        key_total.astype(jnp.bfloat16),
        value_total.astype(jnp.bfloat16),
        grad_table,
    )


def solution(mesh):
    return jax.shard_map(
        on_device,
        mesh=mesh,
        in_specs=(
            P(("grp", "tm", "row"), None),
            P(("grp", "tm", "row"), None),
            P(("grp", "tm", "row"), None),
            P(("grp", "tm", "row"), None),
            P(),
            P(("grp", "tm")),
            P(("grp", "tm", "row"), None),
        ),
        out_specs=(
            P(("grp", "tm", "row"), None),
            P(("grp", "tm", "row"), None),
            P(("grp", "tm", "row"), None),
            P(("grp", "tm", "row"), None),
            P("grp", None),
        ),
        check_vma=False,
    )
```

profile of v0, /device:TPU:0, one launch (start us, length us, event | category | flops | bytes accessed | tf_op | source)
XLA Modules:
  0.0 186.7 jit_solution(2967923302324929908)
XLA Ops:
  8.1 1.0 fusion.14
  10.1 4.9 %collective-permute-start = (bf16[2,128,768]{2,1,0:T(8,128)(2,1)S(1)}, bf16[2,128,768]{2,1,0:T(8,128)(2,1)S(1)}, u32[]{:S(2)}, u32[]{:S(2)}) collective-permute-start(bf16[2,128,768]{2,1,0:T(8,128)(2,1)S(1)} %pad_maximum_fusion.10), channel_id=1, source_target_pairs={{0,2},{2,4},{4,6},{6,8},{8,10},{10,12},{12,14},{1,3},{3,5},{5,7},{... | collective-permute-start | bytes 1179656 | tf_op jit(solution)/shard_map/ppermute | solution.py:16
  16.4 6.9 %collective-permute-done = bf16[2,128,768]{2,1,0:T(8,128)(2,1)S(1)} collective-permute-done((bf16[2,128,768]{2,1,0:T(8,128)(2,1)S(1)}, bf16[2,128,768]{2,1,0:T(8,128)(2,1)S(1)}, u32[]{:S(2)}, u32[]{:S(2)}) %collective-permute-start) | collective-permute-done | bytes 393248 | tf_op jit(solution)/shard_map/ppermute | solution.py:16
  23.3 4.4 %collective-permute-start.1 = (bf16[2,128,768]{2,1,0:T(8,128)(2,1)S(1)}, bf16[2,128,768]{2,1,0:T(8,128)(2,1)S(1)}, u32[]{:S(2)}, u32[]{:S(2)}) collective-permute-start(bf16[2,128,768]{2,1,0:T(8,128)(2,1)S(1)} %collective-permute-done), channel_id=1, source_target_pairs={{0,2},{2,4},{4,6},{6,8},{8,10},{10,12},{12,14},{1,3},{3,5},{5,7},{... | collective-permute-start | bytes 1179656 | tf_op jit(solution)/shard_map/ppermute | solution.py:16
  27.7 2.4 %all_gather.3 = bf16[2,256,768]{2,1,0:T(8,128)(2,1)S(1)} all-gather(bf16[2,128,768]{2,1,0:T(8,128)(2,1)S(1)} %pad_maximum_fusion.10), channel_id=1, replica_groups=mesh['grp'=2,'tm'=8,'row'=2] {'row'}, dimensions={1}, use_global_device_ids=true | all-gather | bytes 1179648 | tf_op jit(solution)/shard_map/all_gather | solution.py:83
  30.1 5.0 %collective-permute-done.1 = bf16[2,128,768]{2,1,0:T(8,128)(2,1)S(1)} collective-permute-done((bf16[2,128,768]{2,1,0:T(8,128)(2,1)S(1)}, bf16[2,128,768]{2,1,0:T(8,128)(2,1)S(1)}, u32[]{:S(2)}, u32[]{:S(2)}) %collective-permute-start.1) | collective-permute-done | bytes 393248 | tf_op jit(solution)/shard_map/ppermute | solution.py:16
  35.2 5.1 %collective-permute-start.2 = (bf16[2,128,768]{2,1,0:T(8,128)(2,1)S(1)}, bf16[2,128,768]{2,1,0:T(8,128)(2,1)}, u32[]{:S(2)}, u32[]{:S(2)}) collective-permute-start(bf16[2,128,768]{2,1,0:T(8,128)(2,1)S(1)} %collective-permute-done.1), channel_id=1, source_target_pairs={{0,2},{2,4},{4,6},{6,8},{8,10},{10,12},{12,14},{1,3},{3,5},{5,7},{... | collective-permute-start | bytes 1179656 | tf_op jit(solution)/shard_map/ppermute | solution.py:16
  43.6 2.5 %collective-permute-done.2 = bf16[2,128,768]{2,1,0:T(8,128)(2,1)} collective-permute-done((bf16[2,128,768]{2,1,0:T(8,128)(2,1)S(1)}, bf16[2,128,768]{2,1,0:T(8,128)(2,1)}, u32[]{:S(2)}, u32[]{:S(2)}) %collective-permute-start.2) | collective-permute-done | bytes 393248 | tf_op jit(solution)/shard_map/ppermute | solution.py:16
  46.1 1.1 pad_maximum_fusion.1
  50.8 1.6 convolution_bitcast_fusion
  52.5 1.1 multiply_reduce_fusion
  55.7 1.0 fusion.27
  57.6 1.2 pad_maximum_fusion
  58.9 1.4 copy-done.2
  61.2 1.3 collective-permute-start.3
  63.8 17.5 %collective-permute-done.3 = f32[2,128,768]{2,1,0:T(8,128)S(1)} collective-permute-done((f32[2,128,768]{2,1,0:T(8,128)S(1)}, f32[2,128,768]{2,1,0:T(8,128)S(1)}, u32[]{:S(2)}, u32[]{:S(2)}) %collective-permute-start.3) | collective-permute-done | bytes 786464 | tf_op jit(solution)/shard_map/ppermute | solution.py:16
  81.4 1.4 collective-permute-start.4
  84.2 17.0 %collective-permute-done.4 = f32[2,128,768]{2,1,0:T(8,128)S(1)} collective-permute-done((f32[2,128,768]{2,1,0:T(8,128)S(1)}, f32[2,128,768]{2,1,0:T(8,128)S(1)}, u32[]{:S(2)}, u32[]{:S(2)}) %collective-permute-start.4) | collective-permute-done | bytes 786464 | tf_op jit(solution)/shard_map/ppermute | solution.py:16
  101.1 1.0 add_add_fusion
  102.2 1.3 collective-permute-start.5
  103.5 1.7 copy.47
  106.4 13.7 %collective-permute-done.5 = f32[2,128,768]{2,1,0:T(8,128)S(1)} collective-permute-done((f32[2,128,768]{2,1,0:T(8,128)}, f32[2,128,768]{2,1,0:T(8,128)S(1)}, u32[]{:S(2)}, u32[]{:S(2)}) %collective-permute-start.5) | collective-permute-done | bytes 786464 | tf_op jit(solution)/shard_map/ppermute | solution.py:16
  120.1 2.0 %fusion.16 = (f32[768]{0:T(1024)S(1)}, bf16[128,768]{1,0:T(8,128)(2,1)}, bf16[128,768]{1,0:T(8,128)(2,1)}) fusion(f32[2,128,768]{2,1,0:T(8,128)S(1)} %collective-permute-done.5, f32[2,128,768]{2,1,0:T(8,128)} %reduce-scatter.2.cloned.1.call-done), kind=kLoop, calls=%fused_computation.41 | loop fusion | flops 490752 | bytes 1969152 | tf_op jit(solution)/shard_map/reduce_sum | solution.py:130
  122.2 57.6 %psum.7 = f32[8,768]{1,0:T(8,128)} all-reduce(f32[8,768]{1,0:T(8,128)S(1)} %broadcast_select_fusion.1), channel_id=1, replica_groups=mesh['grp'=2,'tm'=8,'row'=2] {'tm','row'}, use_global_device_ids=true, to_apply=%region_5.6 | all-reduce | flops 6144 | bytes 49152 | tf_op jit(solution)/shard_map/psum | solution.py:132
  (68 shorter events, 13.5 us)
Async XLA Ops:
  7.2 0.8 copy-start
  7.2 33.1 %copy-start.12 = (s32[1,2]{1,0:T(1,128)S(1)}, s32[1,2]{1,0:T(1,128)}, u32[]{:S(2)}) copy-start(s32[1,2]{1,0:T(1,128)} %param.13) | copy-start | bytes 28
  7.2 35.0 %copy-start.10 = (bf16[128,768]{1,0:T(8,128)(2,1)S(1)}, bf16[128,768]{1,0:T(8,128)(2,1)}, u32[]{:S(2)}) copy-start(bf16[128,768]{1,0:T(8,128)(2,1)} %param.7) | copy-start | bytes 589828
  7.2 112.9 %reduce-scatter.2.cloned.1.call-start = ((), (), s32[]{:S(2)}) async-start(), calls=%async_computation.1 | async-start | bytes 2359296 | tf_op jit(solution)/shard_map/reduce_scatter | solution.py:107
  8.1 34.2 %copy-start.11 = (bf16[128,768]{1,0:T(8,128)(2,1)S(1)}, bf16[128,768]{1,0:T(8,128)(2,1)}, u32[]{:S(2)}) copy-start(bf16[128,768]{1,0:T(8,128)(2,1)} %param.10) | copy-start | bytes 589828
  10.1 13.2 %collective-permute-start = (bf16[2,128,768]{2,1,0:T(8,128)(2,1)S(1)}, bf16[2,128,768]{2,1,0:T(8,128)(2,1)S(1)}, u32[]{:S(2)}, u32[]{:S(2)}) collective-permute-start(bf16[2,128,768]{2,1,0:T(8,128)(2,1)S(1)} %pad_maximum_fusion.10), channel_id=1, source_target_pairs={{0,2},{2,4},{4,6},{6,8},{8,10},{10,12},{12,14},{1,3},{3,5},{5,7},{... | collective-permute-start | bytes 1179656 | tf_op jit(solution)/shard_map/ppermute | solution.py:16
  23.3 11.9 %collective-permute-start.1 = (bf16[2,128,768]{2,1,0:T(8,128)(2,1)S(1)}, bf16[2,128,768]{2,1,0:T(8,128)(2,1)S(1)}, u32[]{:S(2)}, u32[]{:S(2)}) collective-permute-start(bf16[2,128,768]{2,1,0:T(8,128)(2,1)S(1)} %collective-permute-done), channel_id=1, source_target_pairs={{0,2},{2,4},{4,6},{6,8},{8,10},{10,12},{12,14},{1,3},{3,5},{5,7},{... | collective-permute-start | bytes 1179656 | tf_op jit(solution)/shard_map/ppermute | solution.py:16
  35.2 10.9 %collective-permute-start.2 = (bf16[2,128,768]{2,1,0:T(8,128)(2,1)S(1)}, bf16[2,128,768]{2,1,0:T(8,128)(2,1)}, u32[]{:S(2)}, u32[]{:S(2)}) collective-permute-start(bf16[2,128,768]{2,1,0:T(8,128)(2,1)S(1)} %collective-permute-done.1), channel_id=1, source_target_pairs={{0,2},{2,4},{4,6},{6,8},{8,10},{10,12},{12,14},{1,3},{3,5},{5,7},{... | collective-permute-start | bytes 1179656 | tf_op jit(solution)/shard_map/ppermute | solution.py:16
  48.7 1.2 copy-start.3
  50.8 1.6 copy-start.9
  54.1 1.0 copy-start.7
  55.6 1.7 copy-start.1
  58.9 1.4 copy-start.2
  58.9 1.5 copy-start.6
  58.9 1.7 copy-start.5
  61.2 20.1 %collective-permute-start.3 = (f32[2,128,768]{2,1,0:T(8,128)S(1)}, f32[2,128,768]{2,1,0:T(8,128)S(1)}, u32[]{:S(2)}, u32[]{:S(2)}) collective-permute-start(f32[2,128,768]{2,1,0:T(8,128)S(1)} %select_add_fusion), channel_id=1, source_target_pairs={{2,0},{4,2},{6,4},{8,6},{10,8},{12,10},{14,12},{3,1},{5,3},{7,5},{... | collective-permute-start | bytes 2359304 | tf_op jit(solution)/shard_map/ppermute | solution.py:16
  81.4 23.8 %copy-start.4 = (bf16[256,8,96]{0,2,1:T(8,128)(2,1)S(1)}, bf16[256,8,96]{0,2,1:T(8,128)(2,1)}, u32[]{:S(2)}) copy-start(bf16[256,8,96]{0,2,1:T(8,128)(2,1)} %copy-done.3) | copy-start | bytes 1179652
  81.4 23.8 %copy-start.8 = (bf16[8,128,512]{1,2,0:T(8,128)(2,1)S(1)}, bf16[8,128,512]{1,2,0:T(8,128)(2,1)}, u32[]{:S(2)}) copy-start(bf16[8,128,512]{1,2,0:T(8,128)(2,1)} %copy-done.7) | copy-start | bytes 3145732
  81.4 19.7 %collective-permute-start.4 = (f32[2,128,768]{2,1,0:T(8,128)S(1)}, f32[2,128,768]{2,1,0:T(8,128)S(1)}, u32[]{:S(2)}, u32[]{:S(2)}) collective-permute-start(f32[2,128,768]{2,1,0:T(8,128)S(1)} %add_add_fusion.1), channel_id=1, source_target_pairs={{2,0},{4,2},{6,4},{8,6},{10,8},{12,10},{14,12},{3,1},{5,3},{7,5},{... | collective-permute-start | bytes 2359304 | tf_op jit(solution)/shard_map/ppermute | solution.py:16
  102.2 18.0 %collective-permute-start.5 = (f32[2,128,768]{2,1,0:T(8,128)}, f32[2,128,768]{2,1,0:T(8,128)S(1)}, u32[]{:S(2)}, u32[]{:S(2)}) collective-permute-start(f32[2,128,768]{2,1,0:T(8,128)} %add_add_fusion), channel_id=1, source_target_pairs={{2,0},{4,2},{6,4},{8,6},{10,8},{12,10},{14,12},{3,1},{5,3},{7,5},{... | collective-permute-start | bytes 2359304 | tf_op jit(solution)/shard_map/ppermute | solution.py:16
Sparse Core Ops, SparseCore 0:
  59.0 13.1 reduce-scatter.1
where the time goes:
time: 187 us
  waiting for transfers between devices  62.6 us (33%)
  blocking collectives  60 us (32%)
  between operations  19 us (10%)
  starting transfers between devices  18.4 us (10%)
  local copies, waits for them, and re-layouts  11.8 us (6%)
  other arithmetic  10 us (5%)
  matrix products  4.76 us (3%)
    ppermute x6, waiting for transfers between devices, from_behind(): return lax.ppermute(block, axis, route)  62.6 us
    psum x1, blocking collectives, on_device(): grad_table = lax.psum(local_table, ('tm', 'row'))  57.6 us
    ppermute x6, starting transfers between devices, from_behind(): return lax.ppermute(block, axis, route)  18.4 us
    unnamed x30, local copies, waits for them, and re-layouts  5.64 us
  transfers between devices with their start and end apart: 7, of which 6 were waited for; matrix products, arithmetic and copies ran while one was open for 5% of the time, Pallas kernels for 0%

commit v1 on v0

--- a/solution.py
+++ b/solution.py
@@ -129,7 +129,7 @@
     value_total = frame_grads[1] + carried[1]
     column_sums = jnp.sum(value_total, axis=0)
     local_table = jnp.where(matches[:, None], column_sums[None, :], 0.0)
-    grad_table = lax.psum(local_table, ("tm", "row"))
+    grad_table = lax.psum(lax.psum(local_table, "row"), "tm")
     return (
         out_full.astype(jnp.bfloat16),
         grad_query.astype(jnp.bfloat16),

time: 187 us -> 169 us (0.904)
  blocking collectives: 60 us -> 42.1 us
    psum x1 -> x2, blocking collectives: 57.6 us -> 39.7 us  [on_device(): grad_table = lax.psum(lax.psum(local_table, 'row'), 'tm')]
where the time goes in v1:
time: 169 us
  waiting for transfers between devices  62.6 us (37%)
  blocking collectives  42.1 us (25%)
  between operations  19 us (11%)
  starting transfers between devices  18.4 us (11%)
  local copies, waits for them, and re-layouts  11.9 us (7%)
  other arithmetic  10 us (6%)
  matrix products  4.76 us (3%)
    ppermute x6, waiting for transfers between devices, from_behind(): return lax.ppermute(block, axis, route)  62.6 us
    psum x2, blocking collectives, on_device(): grad_table = lax.psum(lax.psum(local_table, 'row'), 'tm')  39.7 us
    ppermute x6, starting transfers between devices, from_behind(): return lax.ppermute(block, axis, route)  18.4 us
    unnamed x30, local copies, waits for them, and re-layouts  5.63 us
  transfers between devices with their start and end apart: 7, of which 6 were waited for; matrix products, arithmetic and copies ran while one was open for 5% of the time, Pallas kernels for 0%

profile of v1, /device:TPU:0, one launch (start us, length us, event | category | flops | bytes accessed | tf_op | source)
XLA Modules:
  0.0 168.8 jit_solution(17642917675835152370)
XLA Ops:
  10.1 4.9 %collective-permute-start = (bf16[2,128,768]{2,1,0:T(8,128)(2,1)S(1)}, bf16[2,128,768]{2,1,0:T(8,128)(2,1)S(1)}, u32[]{:S(2)}, u32[]{:S(2)}) collective-permute-start(bf16[2,128,768]{2,1,0:T(8,128)(2,1)S(1)} %pad_maximum_fusion.10), channel_id=1, source_target_pairs={{0,2},{2,4},{4,6},{6,8},{8,10},{10,12},{12,14},{1,3},{3,5},{5,7},{... | collective-permute-start | bytes 1179656 | tf_op jit(solution)/shard_map/ppermute | solution.py:16
  16.4 6.9 %collective-permute-done = bf16[2,128,768]{2,1,0:T(8,128)(2,1)S(1)} collective-permute-done((bf16[2,128,768]{2,1,0:T(8,128)(2,1)S(1)}, bf16[2,128,768]{2,1,0:T(8,128)(2,1)S(1)}, u32[]{:S(2)}, u32[]{:S(2)}) %collective-permute-start) | collective-permute-done | bytes 393248 | tf_op jit(solution)/shard_map/ppermute | solution.py:16
  23.3 4.4 %collective-permute-start.1 = (bf16[2,128,768]{2,1,0:T(8,128)(2,1)S(1)}, bf16[2,128,768]{2,1,0:T(8,128)(2,1)S(1)}, u32[]{:S(2)}, u32[]{:S(2)}) collective-permute-start(bf16[2,128,768]{2,1,0:T(8,128)(2,1)S(1)} %collective-permute-done), channel_id=1, source_target_pairs={{0,2},{2,4},{4,6},{6,8},{8,10},{10,12},{12,14},{1,3},{3,5},{5,7},{... | collective-permute-start | bytes 1179656 | tf_op jit(solution)/shard_map/ppermute | solution.py:16
  27.7 2.4 %all_gather.3 = bf16[2,256,768]{2,1,0:T(8,128)(2,1)S(1)} all-gather(bf16[2,128,768]{2,1,0:T(8,128)(2,1)S(1)} %pad_maximum_fusion.10), channel_id=1, replica_groups=mesh['grp'=2,'tm'=8,'row'=2] {'row'}, dimensions={1}, use_global_device_ids=true | all-gather | bytes 1179648 | tf_op jit(solution)/shard_map/all_gather | solution.py:83
  30.1 5.0 %collective-permute-done.1 = bf16[2,128,768]{2,1,0:T(8,128)(2,1)S(1)} collective-permute-done((bf16[2,128,768]{2,1,0:T(8,128)(2,1)S(1)}, bf16[2,128,768]{2,1,0:T(8,128)(2,1)S(1)}, u32[]{:S(2)}, u32[]{:S(2)}) %collective-permute-start.1) | collective-permute-done | bytes 393248 | tf_op jit(solution)/shard_map/ppermute | solution.py:16
  35.2 5.1 %collective-permute-start.2 = (bf16[2,128,768]{2,1,0:T(8,128)(2,1)S(1)}, bf16[2,128,768]{2,1,0:T(8,128)(2,1)}, u32[]{:S(2)}, u32[]{:S(2)}) collective-permute-start(bf16[2,128,768]{2,1,0:T(8,128)(2,1)S(1)} %collective-permute-done.1), channel_id=1, source_target_pairs={{0,2},{2,4},{4,6},{6,8},{8,10},{10,12},{12,14},{1,3},{3,5},{5,7},{... | collective-permute-start | bytes 1179656 | tf_op jit(solution)/shard_map/ppermute | solution.py:16
  43.7 2.4 %collective-permute-done.2 = bf16[2,128,768]{2,1,0:T(8,128)(2,1)} collective-permute-done((bf16[2,128,768]{2,1,0:T(8,128)(2,1)S(1)}, bf16[2,128,768]{2,1,0:T(8,128)(2,1)}, u32[]{:S(2)}, u32[]{:S(2)}) %collective-permute-start.2) | collective-permute-done | bytes 393248 | tf_op jit(solution)/shard_map/ppermute | solution.py:16
  46.1 1.1 pad_maximum_fusion.1
  50.8 1.6 convolution_bitcast_fusion
  52.5 1.1 multiply_reduce_fusion
  55.7 1.0 fusion.27
  57.6 1.3 pad_maximum_fusion
  58.9 1.4 copy-done.2
  61.2 1.3 collective-permute-start.3
  63.8 17.5 %collective-permute-done.3 = f32[2,128,768]{2,1,0:T(8,128)S(1)} collective-permute-done((f32[2,128,768]{2,1,0:T(8,128)S(1)}, f32[2,128,768]{2,1,0:T(8,128)S(1)}, u32[]{:S(2)}, u32[]{:S(2)}) %collective-permute-start.3) | collective-permute-done | bytes 786464 | tf_op jit(solution)/shard_map/ppermute | solution.py:16
  81.5 1.4 collective-permute-start.4
  84.2 17.0 %collective-permute-done.4 = f32[2,128,768]{2,1,0:T(8,128)S(1)} collective-permute-done((f32[2,128,768]{2,1,0:T(8,128)S(1)}, f32[2,128,768]{2,1,0:T(8,128)S(1)}, u32[]{:S(2)}, u32[]{:S(2)}) %collective-permute-start.4) | collective-permute-done | bytes 786464 | tf_op jit(solution)/shard_map/ppermute | solution.py:16
  101.1 1.0 add_add_fusion
  102.2 1.3 collective-permute-start.5
  103.5 1.7 %copy.47 = bf16[128,768]{1,0:T(8,128)(2,1)} copy(bf16[128,768]{0,1:T(8,128)(2,1)} %bitcast.99) | data formatting | bytes 393216
  106.4 13.7 %collective-permute-done.5 = f32[2,128,768]{2,1,0:T(8,128)S(1)} collective-permute-done((f32[2,128,768]{2,1,0:T(8,128)}, f32[2,128,768]{2,1,0:T(8,128)S(1)}, u32[]{:S(2)}, u32[]{:S(2)}) %collective-permute-start.5) | collective-permute-done | bytes 786464 | tf_op jit(solution)/shard_map/ppermute | solution.py:16
  120.2 2.0 %fusion.16 = (f32[768]{0:T(1024)S(1)}, bf16[128,768]{1,0:T(8,128)(2,1)}, bf16[128,768]{1,0:T(8,128)(2,1)}) fusion(f32[2,128,768]{2,1,0:T(8,128)S(1)} %collective-permute-done.5, f32[2,128,768]{2,1,0:T(8,128)} %reduce-scatter.2.cloned.1.call-done), kind=kLoop, calls=%fused_computation.41 | loop fusion | flops 490752 | bytes 1969152 | tf_op jit(solution)/shard_map/reduce_sum | solution.py:130
  122.2 3.4 %psum.14 = f32[8,768]{1,0:T(8,128)S(1)} all-reduce(f32[8,768]{1,0:T(8,128)S(1)} %broadcast_select_fusion.1), channel_id=1, replica_groups=mesh['grp'=2,'tm'=8,'row'=2] {'row'}, use_global_device_ids=true, to_apply=%region_5.6 | all-reduce | flops 6144 | bytes 49152 | tf_op jit(solution)/shard_map/psum | solution.py:132
  125.6 36.3 %psum.15 = f32[8,768]{1,0:T(8,128)} all-reduce(f32[8,768]{1,0:T(8,128)S(1)} %psum.14), channel_id=1, replica_groups=mesh['grp'=2,'tm'=8,'row'=2] {'tm'}, use_global_device_ids=true, to_apply=%region_6.7 | all-reduce | flops 6144 | bytes 49152 | tf_op jit(solution)/shard_map/psum | solution.py:132
  (69 shorter events, 14.5 us)
Async XLA Ops:
  7.2 0.8 copy-start
  7.2 33.1 %copy-start.12 = (s32[1,2]{1,0:T(1,128)S(1)}, s32[1,2]{1,0:T(1,128)}, u32[]{:S(2)}) copy-start(s32[1,2]{1,0:T(1,128)} %param.13) | copy-start | bytes 28
  7.2 35.0 %copy-start.10 = (bf16[128,768]{1,0:T(8,128)(2,1)S(1)}, bf16[128,768]{1,0:T(8,128)(2,1)}, u32[]{:S(2)}) copy-start(bf16[128,768]{1,0:T(8,128)(2,1)} %param.7) | copy-start | bytes 589828
  7.2 113.0 %reduce-scatter.2.cloned.1.call-start = ((), (), s32[]{:S(2)}) async-start(), calls=%async_computation.1 | async-start | bytes 2359296 | tf_op jit(solution)/shard_map/reduce_scatter | solution.py:107
  8.1 34.3 %copy-start.11 = (bf16[128,768]{1,0:T(8,128)(2,1)S(1)}, bf16[128,768]{1,0:T(8,128)(2,1)}, u32[]{:S(2)}) copy-start(bf16[128,768]{1,0:T(8,128)(2,1)} %param.10) | copy-start | bytes 589828
  10.1 13.2 %collective-permute-start = (bf16[2,128,768]{2,1,0:T(8,128)(2,1)S(1)}, bf16[2,128,768]{2,1,0:T(8,128)(2,1)S(1)}, u32[]{:S(2)}, u32[]{:S(2)}) collective-permute-start(bf16[2,128,768]{2,1,0:T(8,128)(2,1)S(1)} %pad_maximum_fusion.10), channel_id=1, source_target_pairs={{0,2},{2,4},{4,6},{6,8},{8,10},{10,12},{12,14},{1,3},{3,5},{5,7},{... | collective-permute-start | bytes 1179656 | tf_op jit(solution)/shard_map/ppermute | solution.py:16
  23.3 11.9 %collective-permute-start.1 = (bf16[2,128,768]{2,1,0:T(8,128)(2,1)S(1)}, bf16[2,128,768]{2,1,0:T(8,128)(2,1)S(1)}, u32[]{:S(2)}, u32[]{:S(2)}) collective-permute-start(bf16[2,128,768]{2,1,0:T(8,128)(2,1)S(1)} %collective-permute-done), channel_id=1, source_target_pairs={{0,2},{2,4},{4,6},{6,8},{8,10},{10,12},{12,14},{1,3},{3,5},{5,7},{... | collective-permute-start | bytes 1179656 | tf_op jit(solution)/shard_map/ppermute | solution.py:16
  35.2 10.9 %collective-permute-start.2 = (bf16[2,128,768]{2,1,0:T(8,128)(2,1)S(1)}, bf16[2,128,768]{2,1,0:T(8,128)(2,1)}, u32[]{:S(2)}, u32[]{:S(2)}) collective-permute-start(bf16[2,128,768]{2,1,0:T(8,128)(2,1)S(1)} %collective-permute-done.1), channel_id=1, source_target_pairs={{0,2},{2,4},{4,6},{6,8},{8,10},{10,12},{12,14},{1,3},{3,5},{5,7},{... | collective-permute-start | bytes 1179656 | tf_op jit(solution)/shard_map/ppermute | solution.py:16
  48.7 1.2 copy-start.3
  50.8 1.7 copy-start.9
  54.1 1.0 copy-start.7
  55.6 1.7 %copy-start.1 = (f32[512,8,96]{0,2,1:T(8,128)S(1)}, f32[512,8,96]{0,2,1:T(8,128)}, u32[]{:S(2)}) copy-start(f32[512,8,96]{0,2,1:T(8,128)} %convolution_bitcast_fusion) | copy-start | bytes 4718596
  58.9 1.4 copy-start.2
  58.9 1.5 copy-start.6
  58.9 1.7 copy-start.5
  61.2 20.1 %collective-permute-start.3 = (f32[2,128,768]{2,1,0:T(8,128)S(1)}, f32[2,128,768]{2,1,0:T(8,128)S(1)}, u32[]{:S(2)}, u32[]{:S(2)}) collective-permute-start(f32[2,128,768]{2,1,0:T(8,128)S(1)} %select_add_fusion), channel_id=1, source_target_pairs={{2,0},{4,2},{6,4},{8,6},{10,8},{12,10},{14,12},{3,1},{5,3},{7,5},{... | collective-permute-start | bytes 2359304 | tf_op jit(solution)/shard_map/ppermute | solution.py:16
  81.4 23.8 %copy-start.4 = (bf16[256,8,96]{0,2,1:T(8,128)(2,1)S(1)}, bf16[256,8,96]{0,2,1:T(8,128)(2,1)}, u32[]{:S(2)}) copy-start(bf16[256,8,96]{0,2,1:T(8,128)(2,1)} %copy-done.3) | copy-start | bytes 1179652
  81.4 23.8 %copy-start.8 = (bf16[8,128,512]{1,2,0:T(8,128)(2,1)S(1)}, bf16[8,128,512]{1,2,0:T(8,128)(2,1)}, u32[]{:S(2)}) copy-start(bf16[8,128,512]{1,2,0:T(8,128)(2,1)} %copy-done.7) | copy-start | bytes 3145732
  81.5 19.7 %collective-permute-start.4 = (f32[2,128,768]{2,1,0:T(8,128)S(1)}, f32[2,128,768]{2,1,0:T(8,128)S(1)}, u32[]{:S(2)}, u32[]{:S(2)}) collective-permute-start(f32[2,128,768]{2,1,0:T(8,128)S(1)} %add_add_fusion.1), channel_id=1, source_target_pairs={{2,0},{4,2},{6,4},{8,6},{10,8},{12,10},{14,12},{3,1},{5,3},{7,5},{... | collective-permute-start | bytes 2359304 | tf_op jit(solution)/shard_map/ppermute | solution.py:16
  102.2 18.0 %collective-permute-start.5 = (f32[2,128,768]{2,1,0:T(8,128)}, f32[2,128,768]{2,1,0:T(8,128)S(1)}, u32[]{:S(2)}, u32[]{:S(2)}) collective-permute-start(f32[2,128,768]{2,1,0:T(8,128)} %add_add_fusion), channel_id=1, source_target_pairs={{2,0},{4,2},{6,4},{8,6},{10,8},{12,10},{14,12},{3,1},{5,3},{7,5},{... | collective-permute-start | bytes 2359304 | tf_op jit(solution)/shard_map/ppermute | solution.py:16
Sparse Core Ops, SparseCore 0:
  59.1 13.1 reduce-scatter.1
